TPU v7x, 1024 devices: a whole 8x8x8 slice. The times are simulated.
1024 devices in a mesh: slab: 16 (over x_hi, y), sample: 64 (over z, x_lo, core).
Axes of the slice: x: 8 (x_hi: 2, x_lo: 4; x = x_hi * 4 + x_lo), y: 8, z: 8, core: 2. Of those that a mesh axis runs over, the one named last changes fastest.
Arguments:
- activations: bfloat16 [64, 32, 64, 8, 128], P('sample', None, 'slab'), may hold values from -6 to 6
- grad_out: bfloat16 [64, 64, 64, 8, 128], P('sample', 'slab'), may hold values from -6 to 6
- weight: bfloat16 [27, 64, 32], replicated, may hold values from -0.21875 to 0.21875
Outputs:
- grad_inputs: bfloat16 [64, 32, 64, 8, 128], P('sample', None, 'slab')
- grad_weight: float32 [27, 64, 32], replicated
- grad_bias: float32 [64], replicated
All inputs are finite; a program needn't handle non-finite values.
Results may differ from a plain program's by a relative error of at most 0.001.
Values may be sent and summed in bfloat16 or wider, within the bound.
A program may use at most 32 MiB of HBM per device.

v0:
```python
import math

import jax
import jax.numpy as jnp
from jax import lax
from jax.sharding import PartitionSpec as P


def with_halo(block, sides, width):
    for axis, dim in sides:
        count = lax.axis_size(axis)
        forward = [(i, i + 1) for i in range(count - 1)]
        backward = [(target, source) for source, target in forward]
        low = lax.ppermute(
            lax.slice_in_dim(block, block.shape[dim] - width, None, axis=dim), axis, forward
        )
        high = lax.ppermute(lax.slice_in_dim(block, 0, width, axis=dim), axis, backward)
        block = jnp.concatenate([low, block, high], axis=dim)
    return block


def offsets_list():
    return [
        (shift_z, shift_y, shift_x)
        for shift_z in (-1, 0, 1)
        for shift_y in (-1, 0, 1)
        for shift_x in (-1, 0, 1)
    ]


def local(activations, grad_out, weight):
    samples, in_chan, planes, y_cells, x_cells = activations.shape
    slabs = lax.axis_size("slab")
    x_ext = with_halo(activations, (("slab", 2),), 1)
    regrouped = lax.all_to_all(grad_out, "slab", split_axis=2, concat_axis=1, tiled=True)
    g_ext = with_halo(regrouped, (("slab", 2),), 1)
    widths = ((0, 0), (0, 0), (0, 0), (1, 1), (1, 1))
    padded_in = jnp.pad(x_ext, widths)
    padded_co = jnp.pad(g_ext, widths)
    center = padded_co[:, :, 1 : 1 + planes, 1 : 1 + y_cells, 1 : 1 + x_cells]
    grad_in = jnp.zeros((samples, in_chan, planes, y_cells, x_cells), jnp.float32)
    pieces = []
    for offset, (shift_z, shift_y, shift_x) in enumerate(offsets_list()):
        moved_in = padded_in[
            :,
            :,
            1 + shift_z : 1 + shift_z + planes,
            1 + shift_y : 1 + shift_y + y_cells,
            1 + shift_x : 1 + shift_x + x_cells,
        ]
        moved_co = padded_co[
            :,
            :,
            1 - shift_z : 1 - shift_z + planes,
            1 - shift_y : 1 - shift_y + y_cells,
            1 - shift_x : 1 - shift_x + x_cells,
        ]
        pieces.append(
            jnp.einsum("sozyx,sizyx->oi", center, moved_in, preferred_element_type=jnp.float32)
        )
        grad_in = grad_in + jnp.einsum(
            "oi,sozyx->sizyx", weight[offset], moved_co, preferred_element_type=jnp.float32
        )
    wpart = jnp.stack(pieces)
    bpart = jnp.sum(center.astype(jnp.float32), axis=(0, 2, 3, 4))
    wtotal, btotal = lax.psum((wpart, bpart), ("slab", "sample"))
    all_cells = samples * lax.axis_size("sample") * planes * slabs * y_cells * x_cells
    factor = 1.0 / math.sqrt(all_cells)
    return (grad_in.astype(jnp.bfloat16), wtotal * factor, btotal * factor)


def solution(mesh):
    placed = (P("sample", None, "slab", None, None), P("sample", "slab", None, None, None), P())
    return jax.shard_map(
        local,
        mesh=mesh,
        in_specs=placed,
        out_specs=(P("sample", None, "slab", None, None), P(), P()),
        check_vma=False,
    )
```

profile of v0, /device:TPU:1, one launch (start us, length us, event | category | flops | bytes accessed | tf_op | source)
XLA Modules:
  0.0 479.7 jit_solution(6631201099331581678)
XLA Ops:
  7.2 2.0 copy.76
  9.1 13.1 %all-to-all-start = ((bf16[1,4,64,8,128]{4,3,1,0,2:T(8,128)(2,1)}), bf16[1,4,64,8,128]{4,3,1,0,2:T(8,128)(2,1)S(1)}, u32[]{:S(2)}, u32[]{:S(2)}) async-start(bf16[1,4,64,8,128]{4,3,1,0,2:T(8,128)(2,1)} %copy.76), calls=%async_computation | async-start | bytes 1048576 | tf_op jit(solution)/shard_map/all_to_all | solution.py:35
  22.5 3.3 collective-permute-start.2
  25.7 1.3 collective-permute-start.3
  27.0 0.4 collective-permute-done.2
  27.4 8.3 %collective-permute-done.3 = bf16[1,32,1,8,128]{4,1,2,3,0:T(8,128)(2,1)S(1)} collective-permute-done((bf16[1,32,1,8,128]{4,1,2,3,0:T(8,128)(2,1)S(1)}, bf16[1,32,1,8,128]{4,1,2,3,0:T(8,128)(2,1)S(1)}, u32[]{:S(2)}, u32[]{:S(2)}) %collective-permute-start.3) | collective-permute-done | bytes 65568 | tf_op jit(solution)/shard_map/ppermute | solution.py:17
  35.7 0.4 select_maximum_fusion.2
  36.8 131.6 %psum.15 = f32[64]{0:T(128)S(1)} all-reduce(f32[64]{0:T(128)S(1)} %reduce_sum.12), channel_id=1, replica_groups=mesh['slab'=16,'sample'=64] {'slab','sample'}, use_global_device_ids=true, to_apply=%region_2.3 | all-reduce | flops 64 | bytes 512 | tf_op jit(solution)/shard_map/psum | solution.py:66
  168.3 0.5 broadcast_multiply_fusion.1
  168.9 1.9 collective-permute-start
  170.8 1.5 collective-permute-start.1
  180.4 0.8 copy-done
  181.4 279.7 %all-reduce.4.cloned.1.call-done = f32[27,64,32]{1,2,0:T(8,128)} async-done(((f32[27,64,32]{1,2,0:T(8,128)}), f32[27,64,32]{1,2,0:T(8,128)}) %all-reduce.4.cloned.1.call-update) | async-done | bytes 221200 | tf_op jit(solution)/shard_map/psum | solution.py:66
  461.1 1.8 broadcast_multiply_fusion
  462.9 1.1 select_maximum_fusion
  464.9 0.4 fusion.72
  465.3 0.4 fusion.73
  465.9 0.4 fusion.75
  466.8 0.4 fusion.82
  467.4 0.4 fusion.84
  467.9 0.6 fusion.34
  469.8 0.4 fusion.16
  471.5 0.4 fusion.10
  472.1 0.8 copy.111
  (62 shorter events, 14.1 us)
Async XLA Ops:
  7.2 15.2 %copy-start.1 = (bf16[1,32,4,8,128]{4,3,2,1,0:T(8,128)(2,1)S(1)}, bf16[1,32,4,8,128]{4,3,2,1,0:T(8,128)(2,1)}, u32[]{:S(2)}) copy-start(bf16[1,32,4,8,128]{4,3,2,1,0:T(8,128)(2,1)} %param.3) | copy-start | bytes 786436
  9.1 27.0 %all-to-all-start = ((bf16[1,4,64,8,128]{4,3,1,0,2:T(8,128)(2,1)}), bf16[1,4,64,8,128]{4,3,1,0,2:T(8,128)(2,1)S(1)}, u32[]{:S(2)}, u32[]{:S(2)}) async-start(bf16[1,4,64,8,128]{4,3,1,0,2:T(8,128)(2,1)} %copy.76), calls=%async_computation | async-start | bytes 1048576 | tf_op jit(solution)/shard_map/all_to_all | solution.py:35
  22.3 438.8 %all-reduce.4.cloned.1.call-start = ((), (), s32[]{:S(2)}) async-start(), calls=%async_computation.1 | async-start | bytes 884736 | tf_op jit(solution)/shard_map/psum | solution.py:66
  22.5 4.9 %collective-permute-start.2 = (bf16[1,32,1,8,128]{4,1,2,3,0:T(8,128)(2,1)S(1)}, bf16[1,32,1,8,128]{4,1,2,3,0:T(8,128)(2,1)S(1)}, u32[]{:S(2)}, u32[]{:S(2)}) collective-permute-start(bf16[1,32,1,8,128]{4,1,2,3,0:T(8,128)(2,1)S(1)} %get-tuple-element.14), channel_id=1, source_target_pairs={{0,64},{64,128},{128,192},{192,256},{256,320},{320,384},{384,448},... | collective-permute-start | bytes 196616 | tf_op jit(solution)/shard_map/ppermute | solution.py:14
  25.7 10.0 %collective-permute-start.3 = (bf16[1,32,1,8,128]{4,1,2,3,0:T(8,128)(2,1)S(1)}, bf16[1,32,1,8,128]{4,1,2,3,0:T(8,128)(2,1)S(1)}, u32[]{:S(2)}, u32[]{:S(2)}) collective-permute-start(bf16[1,32,1,8,128]{4,1,2,3,0:T(8,128)(2,1)S(1)} %get-tuple-element.15), channel_id=1, source_target_pairs={{64,0},{128,64},{192,128},{256,192},{320,256},{384,320},{448,384},... | collective-permute-start | bytes 196616 | tf_op jit(solution)/shard_map/ppermute | solution.py:17
  168.9 294.1 %collective-permute-start = (bf16[1,64,1,8,128]{4,1,3,2,0:T(8,128)(2,1)S(1)}, bf16[1,64,1,8,128]{4,1,3,2,0:T(8,128)(2,1)S(1)}, u32[]{:S(2)}, u32[]{:S(2)}) collective-permute-start(bf16[1,64,1,8,128]{4,1,3,2,0:T(8,128)(2,1)S(1)} %get-tuple-element.12), channel_id=1, source_target_pairs={{0,64},{64,128},{128,192},{192,256},{256,320},{320,384},{384,448},... | collective-permute-start | bytes 393224 | tf_op jit(solution)/shard_map/ppermute | solution.py:14
  170.8 292.1 %collective-permute-start.1 = (bf16[1,64,1,8,128]{4,1,3,2,0:T(8,128)(2,1)S(1)}, bf16[1,64,1,8,128]{4,1,3,2,0:T(8,128)(2,1)S(1)}, u32[]{:S(2)}, u32[]{:S(2)}) collective-permute-start(bf16[1,64,1,8,128]{4,1,3,2,0:T(8,128)(2,1)S(1)} %get-tuple-element.13), channel_id=1, source_target_pairs={{64,0},{128,64},{192,128},{256,192},{320,256},{384,320},{448,384},... | collective-permute-start | bytes 393224 | tf_op jit(solution)/shard_map/ppermute | solution.py:17
  179.2 2.1 copy-start.2
  180.4 0.8 copy-start
Sparse Core Ops, SparseCore 0:
  181.3 279.7 all-reduce.3
where the time goes:
time: 480 us
  waiting for transfers between devices  288 us (60%)
  blocking collectives  132 us (28%)
  starting transfers between devices  21.1 us (4%)
  matrix products  16.3 us (3%)
  between operations  14.2 us (3%)
    psum x1, waiting for transfers between devices, local(): wtotal, btotal = lax.psum((wpart, bpart), ('slab', 'sample'))  280 us
    psum x1, blocking collectives, local(): wtotal, btotal = lax.psum((wpart, bpart), ('slab', 'sample'))  132 us
    all_to_all x1, starting transfers between devices, local(): lax.all_to_all(grad_out, 'slab', split_axis=2, concat_axis=1, tiled=True)  13.1 us
  transfers between devices with their start and end apart: 6, of which 3 were waited for; matrix products, arithmetic and copies ran while one was open for 2% of the time, Pallas kernels for 0%

commit v1 on v0

v1 whole, which is shorter than its diff:
```python
import functools
import math

import jax
import jax.numpy as jnp
from jax import lax
from jax.experimental import pallas as pl
from jax.experimental.pallas import tpu as pltpu
from jax.sharding import PartitionSpec as P

MESH = pl.DeviceIdType.MESH
F32 = jnp.float32
BF16 = jnp.bfloat16


def lane_shift(value, shift):
    lane = lax.broadcasted_iota(jnp.int32, value.shape, value.ndim - 1)
    rolled = pltpu.roll(value, shift % 128, value.ndim - 1)
    edge = 0 if shift > 0 else 127
    return jnp.where(lane == edge, 0.0, rolled)


def compute_kernel(g_ref, a_ref, w_ref, gi_ref, gw_ref, g_pad, a_stack, w_rows, acc):
    chans, planes_ext, rows, lanes = g_ref.shape
    in_chan, planes = a_ref.shape[:2]
    g_pad[:, 0] = jnp.zeros((planes_ext, chans, lanes), BF16)
    g_pad[:, rows + 1] = jnp.zeros((planes_ext, chans, lanes), BF16)
    for z in range(planes_ext):
        plane = g_ref[:, z].astype(F32)
        g_pad[z, 1 : rows + 1] = jnp.swapaxes(plane, 0, 1).astype(BF16)
    tail = lax.broadcasted_iota(jnp.int32, (rows, 32, lanes), 1) == 0
    for z in range(planes):
        cells = jnp.swapaxes(a_ref[:, z].astype(F32), 0, 1)
        stack = [lane_shift(cells, 1), cells, lane_shift(cells, -1), jnp.where(tail, 1.0, 0.0)]
        for part, value in enumerate(stack):
            a_stack[z * rows : (z + 1) * rows, part * 32 : part * 32 + 32] = value.astype(BF16)
    for zy in range(9):
        joined = jnp.concatenate([w_ref[3 * zy + dx].astype(F32) for dx in range(3)], axis=1)
        w_rows[:, zy * chans : (zy + 1) * chans] = joined.T.astype(BF16)
    acc[...] = jnp.zeros_like(acc)
    for z in range(planes):
        outs = []
        for y in range(0, rows, 2):
            blocks = []
            for dz in (-1, 0, 1):
                for dy in (-1, 0, 1):
                    blocks.append(
                        jnp.concatenate(
                            [g_pad[z + 1 - dz, y + 1 - dy], g_pad[z + 1 - dz, y + 2 - dy]], axis=1
                        )
                    )
            stacked = jnp.concatenate(blocks, axis=0)
            cells = jnp.concatenate([a_stack[z * rows + y], a_stack[z * rows + y + 1]], axis=1)
            acc[...] += lax.dot_general(
                stacked, cells, (((1,), (1,)), ((), ())), preferred_element_type=F32
            )
            mixed = jnp.dot(w_rows[...], stacked, preferred_element_type=F32)
            for half in range(2):
                part = mixed[:, half * lanes : (half + 1) * lanes]
                outs.append(
                    part[32:64] + lane_shift(part[0:32], -1) + lane_shift(part[64:96], 1)
                )
        gi_ref[:, z] = jnp.swapaxes(jnp.stack(outs), 0, 1).astype(BF16)
    for block in range(gw_ref.shape[0]):
        gw_ref[block] = acc[block * 4 : block * 4 + 4]


def compute(g_ext, activations, weight):
    chans, planes_ext, rows, lanes = g_ext.shape
    in_chan, planes = activations.shape[:2]
    vmem = pl.BlockSpec(memory_space=pltpu.VMEM)
    return pl.pallas_call(
        compute_kernel,
        out_shape=(
            jax.ShapeDtypeStruct(activations.shape, BF16),
            jax.ShapeDtypeStruct((144, 4, 128), F32),
        ),
        in_specs=[vmem] * 3,
        out_specs=(vmem, vmem),
        scratch_shapes=[
            pltpu.VMEM((planes_ext, rows + 2, chans, lanes), BF16),
            pltpu.VMEM((planes * rows, 128, lanes), BF16),
            pltpu.VMEM((96, 9 * chans), BF16),
            pltpu.VMEM((9 * chans, 128), F32),
        ],
        compiler_params=pltpu.CompilerParams(vmem_limit_bytes=48 << 20),
        name="products",
    )(g_ext, activations, weight)


def reduce_kernel(n, factor, x_ref, out_ref, first, second, third, send_sem, recv_sem):
    half = n // 2
    members = 2 * n
    unit = x_ref.shape[0] // (3 * members)
    slab, sample = lax.axis_index("slab"), lax.axis_index("sample")
    core = sample % 2
    place = (
        (slab // n) * half + (sample // 2) % half,
        slab % n,
        sample // n,
    )

    def device(axis, coordinate, other):
        x, y, z = (coordinate if axis == i else place[i] for i in range(3))
        return {"slab": (x // half) * n + y, "sample": z * n + (x % half) * 2 + other}

    def wide(axis, step):
        index = (place[axis] * 2 + core + step) % members
        return index, device(axis, index // 2, index % 2)

    def narrow(axis, step):
        index = (place[axis] + step) % n
        return index, device(axis, index, core)

    barrier = pltpu.get_barrier_semaphore()
    for axis in range(3):

        @pl.loop(1, members)
        def _(step, axis=axis):
            pl.semaphore_signal(
                barrier, inc=1, device_id=wide(axis, step)[1], device_id_type=MESH
            )

    pl.semaphore_wait(barrier, 3 * (members - 1))

    def copy(source, target, phase, part, peer):
        return pltpu.make_async_remote_copy(
            src_ref=source,
            dst_ref=target,
            send_sem=send_sem.at[phase, part],
            recv_sem=recv_sem.at[phase, part],
            device_id=peer,
            device_id_type=MESH,
        )

    def whole(buffer, count, sem):
        pltpu.make_async_copy(buffer.at[pl.ds(0, count)], buffer.at[pl.ds(0, count)], sem).wait()

    own = [place[part] * 2 + core for part in range(3)]
    for part in range(3):

        @pl.loop(1, members)
        def _(step, part=part):
            index, peer = wide(part, step)
            copy(
                x_ref.at[pl.ds((part * members + index) * unit, unit)],
                first.at[part, pl.ds(own[part] * unit, unit)],
                0,
                part,
                peer,
            ).start()

    for part in range(3):
        first[part, pl.ds(own[part] * unit, unit)] = x_ref[
            pl.ds((part * members + own[part]) * unit, unit)
        ]
        whole(first.at[part], (members - 1) * unit, recv_sem.at[0, part])
        total = first[part, pl.ds(0, unit)]
        for index in range(1, members):
            total = total + first[part, pl.ds(index * unit, unit)]
        axis = (part + 1) % 3
        mine = pl.ds(place[axis] * unit, unit)
        second[part, mine] = total

        @pl.loop(1, n)
        def _(step, part=part, axis=axis, mine=mine):
            copy(second.at[part, mine], second.at[part, mine], 1, part, narrow(axis, step)[1]).start()

    for part in range(3):
        whole(second.at[part], (n - 1) * unit, recv_sem.at[1, part])
        total = second[part, pl.ds(0, unit)]
        for index in range(1, n):
            total = total + second[part, pl.ds(index * unit, unit)]
        axis = (part + 2) % 3
        mine = pl.ds(place[axis] * unit, unit)
        third[part, mine] = total

        @pl.loop(1, n)
        def _(step, part=part, axis=axis, mine=mine):
            copy(third.at[part, mine], third.at[part, mine], 2, part, narrow(axis, step)[1]).start()

    for part in range(3):
        whole(third.at[part], (n - 1) * unit, recv_sem.at[2, part])
        total = third[part, pl.ds(0, unit)]
        for index in range(1, n):
            total = total + third[part, pl.ds(index * unit, unit)]
        mine = pl.ds((part * members + own[part]) * unit, unit)
        out_ref[mine] = total * factor

        @pl.loop(1, members)
        def _(step, part=part, mine=mine):
            copy(out_ref.at[mine], out_ref.at[mine], 3, part, wide(part, step)[1]).start()

    for part in range(3):
        whole(out_ref, (members - 1) * unit, recv_sem.at[3, part])
    for part in range(3):
        whole(out_ref, (members - 1) * unit, send_sem.at[0, part])
        whole(out_ref, (n - 1) * unit, send_sem.at[1, part])
        whole(out_ref, (n - 1) * unit, send_sem.at[2, part])
        whole(out_ref, (members - 1) * unit, send_sem.at[3, part])


def reduce_all(partial, n, factor):
    members = 2 * n
    unit = partial.shape[0] // (3 * members)
    vmem = pl.BlockSpec(memory_space=pltpu.VMEM)
    return pl.pallas_call(
        functools.partial(reduce_kernel, n, factor),
        out_shape=jax.ShapeDtypeStruct(partial.shape, F32),
        in_specs=[vmem],
        out_specs=vmem,
        scratch_shapes=[
            pltpu.VMEM((3, members * unit, 4, 128), F32),
            pltpu.VMEM((3, n * unit, 4, 128), F32),
            pltpu.VMEM((3, n * unit, 4, 128), F32),
            pltpu.SemaphoreType.DMA((4, 3)),
            pltpu.SemaphoreType.DMA((4, 3)),
        ],
        compiler_params=pltpu.CompilerParams(collective_id=0, has_side_effects=True),
        name="total",
    )(partial)


def local(activations, grad_out, weight):
    slabs, samples = lax.axis_size("slab"), lax.axis_size("sample")
    planes = activations.shape[2]
    regrouped = lax.all_to_all(grad_out, "slab", split_axis=2, concat_axis=1, tiled=True)
    up = [(i, i + 1) for i in range(slabs - 1)]
    down = [(i + 1, i) for i in range(slabs - 1)]
    low = lax.ppermute(regrouped[:, :, planes - 1 :], "slab", up)
    high = lax.ppermute(regrouped[:, :, :1], "slab", down)
    g_ext = jnp.concatenate([low, regrouped, high], axis=2)
    grad_in, partial = compute(g_ext[0], activations[0], weight)
    cells = samples * slabs * math.prod(activations.shape[2:])
    total = reduce_all(partial, slabs // 2, 1.0 / math.sqrt(cells))
    total = total.reshape(9, 64, 128)
    gw = total[:, :, :96].reshape(9, 64, 3, 32).transpose(0, 2, 1, 3).reshape(27, 64, 32)
    return grad_in[None], gw, total[4, :, 96]


def solution(mesh):
    placed = (P("sample", None, "slab", None, None), P("sample", "slab", None, None, None), P())
    return jax.shard_map(
        local,
        mesh=mesh,
        in_specs=placed,
        out_specs=(P("sample", None, "slab", None, None), P(), P()),
        check_vma=False,
    )
```

time: 480 us -> 104 us (0.22)
  waiting for transfers between devices: 288 us -> 1.64 us
  blocking collectives: 132 us -> 26.3 us
  Pallas kernels: 0 us -> 62.7 us
  matrix products: 16.3 us -> 0 us
  starting transfers between devices: 21.1 us -> 5.42 us
  between operations: 14.2 us -> 0.75 us
    psum x1 -> x0, waiting for transfers between devices: 280 us -> none  [local(): wtotal, btotal = lax.psum((wpart, bpart), ('slab', 'sample'))]
    psum x1 -> x0, blocking collectives: 132 us -> none  [local(): wtotal, btotal = lax.psum((wpart, bpart), ('slab', 'sample'))]
    pallas_call x0 -> x2, Pallas kernels: none -> 62.7 us  [the longest x1 59.3 us: reduce_all(): pl.pallas_call(functools.partial(reduce_kernel, n, factor), out_shape=jax...]
    all_to_all x0 -> x1, blocking collectives: none -> 26.3 us  [local(): lax.all_to_all(grad_out, 'slab', split_axis=2, concat_axis=1, tiled=True)]
    dot_general x54 -> x0, matrix products: 16.3 us -> none  [the longest x27 8.22 us: local(): jnp.einsum('oi,sozyx->sizyx', weight[offset], moved_co, preferred_element...]
    all_to_all x1 -> x0, starting transfers between devices: 13.1 us -> none  [local(): lax.all_to_all(grad_out, 'slab', split_axis=2, concat_axis=1, tiled=True)]
    ppermute x4 -> x2, waiting for transfers between devices: 8.66 us -> 1.64 us  [the longest x1 1.51 us: local(): low = lax.ppermute(regrouped[:, :, planes - 1:], 'slab', up)]
  transfers between devices with their start and end apart: 6 -> 2, of which waited for: 3 -> 2; matrix products, arithmetic and copies ran while one was open for 2% -> 0% of each run, Pallas kernels for 0% -> 0%
where the time goes in v1:
time: 104 us
  Pallas kernels  62.7 us (60%)
  blocking collectives  26.3 us (25%)
  local copies, waits for them, and re-layouts  6.85 us (7%)
  starting transfers between devices  5.42 us (5%)
  waiting for transfers between devices  1.64 us (2%)
    pallas_call x1, Pallas kernels, reduce_all(): pl.pallas_call(functools.partial(reduce_kernel, n, factor), out_shape=jax...  59.3 us
    all_to_all x1, blocking collectives, local(): lax.all_to_all(grad_out, 'slab', split_axis=2, concat_axis=1, tiled=True)  26.3 us
    unnamed x13, local copies, waits for them, and re-layouts  4.37 us
    ppermute x1, starting transfers between devices, local(): low = lax.ppermute(regrouped[:, :, planes - 1:], 'slab', up)  3.99 us
    pallas_call x1, Pallas kernels, compute(): pl.pallas_call(compute_kernel, out_shape=(jax.ShapeDtypeStruct(activation...  3.44 us
  transfers between devices with their start and end apart: 2, of which 2 were waited for; matrix products, arithmetic and copies ran while one was open for 0% of the time, Pallas kernels for 0%

profile of v1, /device:TPU:1, one launch (start us, length us, event | category | flops | bytes accessed | tf_op | source)
XLA Modules:
  0.0 104.0 jit_solution(7199760789023945791)
XLA Ops:
  0.6 1.1 %copy.16 = bf16[1,4,64,8,128]{4,3,1,0,2:T(8,128)(2,1)S(1)} copy(bf16[1,4,64,8,128]{4,3,2,1,0:T(8,128)(2,1)} %param.4) | data formatting | bytes 1048576 | tf_op args[1]
  1.8 26.3 %all_to_all.18 = bf16[1,4,64,8,128]{4,3,1,0,2:T(8,128)(2,1)S(1)} all-to-all(bf16[1,4,64,8,128]{4,3,1,0,2:T(8,128)(2,1)S(1)} %copy.16), channel_id=1, replica_groups=mesh['slab'=16,'sample'=64] {'slab'}, dimensions={2} | all-to-all | bytes 1048576 | tf_op jit(solution)/shard_map/all_to_all | solution.py:227
  28.1 0.1 copy.17
  28.2 0.0 copy-start.2
  28.2 1.4 %collective-permute-start.1 = (bf16[1,64,1,8,128]{4,3,2,1,0:T(8,128)(2,1)S(1)}, bf16[1,64,1,8,128]{4,3,2,1,0:T(8,128)(2,1)S(1)}, u32[]{:S(2)}, u32[]{:S(2)}) collective-permute-start(bf16[1,64,1,8,128]{4,3,2,1,0:T(8,128)(2,1)S(1)} %get-tuple-element.14), channel_id=1, source_target_pairs={{64,0},{128,64},{192,128},{256,192},{320,256},{384,320},{448,384},... | collective-permute-start | bytes 393224 | tf_op jit(solution)/shard_map/ppermute | solution.py:231
  29.6 4.0 %collective-permute-start = (bf16[1,64,1,8,128]{4,3,2,1,0:T(8,128)(2,1)S(1)}, bf16[1,64,1,8,128]{4,3,2,1,0:T(8,128)(2,1)S(1)}, u32[]{:S(2)}, u32[]{:S(2)}) collective-permute-start(bf16[1,64,1,8,128]{4,3,2,1,0:T(8,128)(2,1)S(1)} %get-tuple-element.13), channel_id=1, source_target_pairs={{0,64},{64,128},{128,192},{192,256},{256,320},{320,384},{384,448},... | collective-permute-start | bytes 393224 | tf_op jit(solution)/shard_map/ppermute | solution.py:230
  33.7 0.3 copy.18.w_ref
  33.9 0.0 copy-start.1
  33.9 0.1 collective-permute-done.1
  34.1 1.5 %collective-permute-done = bf16[1,64,1,8,128]{4,3,2,1,0:T(8,128)(2,1)S(1)} collective-permute-done((bf16[1,64,1,8,128]{4,3,2,1,0:T(8,128)(2,1)S(1)}, bf16[1,64,1,8,128]{4,3,2,1,0:T(8,128)(2,1)S(1)}, u32[]{:S(2)}, u32[]{:S(2)}) %collective-permute-start) | collective-permute-done | bytes 131104 | tf_op jit(solution)/shard_map/ppermute | solution.py:230
  35.6 0.1 maximum_bitcast_fusion.g_ref
  35.7 0.0 copy-done.1
  35.7 3.4 %products.1 = (bf16[32,4,8,128]{3,2,1,0:T(8,128)(2,1)}, f32[144,4,128]{2,1,0:T(4,128)S(1)}) custom-call(bf16[64,6,8,128]{3,2,1,0:T(8,128)(2,1)S(1)} %maximum_bitcast_fusion.g_ref, bf16[32,4,8,128]{3,2,1,0:T(8,128)(2,1)S(1)} %bitcast.12, bf16[27,64,32]{2,1,0:T(8,128)(2,1)S(1)} %copy.18.w_ref), custom_call_target="tpu_custom_call" | custom-call | tf_op jit(solution)/shard_map/products/pallas_call | solution.py:72
  39.2 0.7 copy-done
  39.9 59.3 %total.1 = f32[144,4,128]{2,1,0:T(4,128)} custom-call(f32[144,4,128]{2,1,0:T(4,128)} %copy-done), custom_call_target="tpu_custom_call" | custom-call | tf_op jit(solution)/shard_map/total/pallas_call | solution.py:207
  99.2 1.4 %fusion.1 = (f32[9,64,32]{2,1,0:T(8,128)S(1)}, f32[9,64,32]{2,1,0:T(8,128)S(1)}, f32[9,64,32]{2,1,0:T(8,128)S(1)}) fusion(f32[9,64,128]{2,1,0:T(8,128)} %bitcast.13), kind=kLoop, calls=%fused_computation.3 | loop fusion | bytes 442368 | tf_op jit(solution)/shard_map/slice
  100.6 0.8 slice.33
  101.4 0.2 copy.26
  101.7 0.2 copy.25
  101.9 0.2 copy.24
  102.1 0.2 pad_maximum_fusion
  102.3 0.1 reshape.14
  102.4 1.0 copy.23
  103.5 0.6 copy.27
  (3 shorter events, 0.0 us)
Async XLA Ops:
  28.2 5.5 %copy-start.2 = (bf16[27,64,32]{1,2,0:T(8,128)(2,1)S(1)}, bf16[27,64,32]{1,2,0:T(8,128)(2,1)}, u32[]{:S(2)}) copy-start(bf16[27,64,32]{1,2,0:T(8,128)(2,1)} %param.5) | copy-start | bytes 331780
  28.2 5.8 %collective-permute-start.1 = (bf16[1,64,1,8,128]{4,3,2,1,0:T(8,128)(2,1)S(1)}, bf16[1,64,1,8,128]{4,3,2,1,0:T(8,128)(2,1)S(1)}, u32[]{:S(2)}, u32[]{:S(2)}) collective-permute-start(bf16[1,64,1,8,128]{4,3,2,1,0:T(8,128)(2,1)S(1)} %get-tuple-element.14), channel_id=1, source_target_pairs={{64,0},{128,64},{192,128},{256,192},{320,256},{384,320},{448,384},... | collective-permute-start | bytes 393224 | tf_op jit(solution)/shard_map/ppermute | solution.py:231
  29.6 5.9 %collective-permute-start = (bf16[1,64,1,8,128]{4,3,2,1,0:T(8,128)(2,1)S(1)}, bf16[1,64,1,8,128]{4,3,2,1,0:T(8,128)(2,1)S(1)}, u32[]{:S(2)}, u32[]{:S(2)}) collective-permute-start(bf16[1,64,1,8,128]{4,3,2,1,0:T(8,128)(2,1)S(1)} %get-tuple-element.13), channel_id=1, source_target_pairs={{0,64},{64,128},{128,192},{192,256},{256,320},{320,384},{384,448},... | collective-permute-start | bytes 393224 | tf_op jit(solution)/shard_map/ppermute | solution.py:230
  33.9 1.8 %copy-start.1 = (bf16[1,32,4,8,128]{4,3,2,1,0:T(8,128)(2,1)S(1)}, bf16[1,32,4,8,128]{4,3,2,1,0:T(8,128)(2,1)}, u32[]{:S(2)}) copy-start(bf16[1,32,4,8,128]{4,3,2,1,0:T(8,128)(2,1)} %param.3) | copy-start | bytes 786436
  39.2 0.7 copy-start

commit v2 on v0

v2 whole, which is shorter than its diff:
```python
import functools
import math

import jax
import jax.numpy as jnp
from jax import lax
from jax.experimental import pallas as pl
from jax.experimental.pallas import tpu as pltpu
from jax.sharding import PartitionSpec as P

MESH = pl.DeviceIdType.MESH
F32 = jnp.float32
BF16 = jnp.bfloat16


def lane_shift(value, shift):
    lane = lax.broadcasted_iota(jnp.int32, value.shape, value.ndim - 1)
    rolled = pltpu.roll(value, shift % 128, value.ndim - 1)
    edge = 0 if shift > 0 else 127
    return jnp.where(lane == edge, 0.0, rolled)


def far_out(middle, send):
    send(middle)

    @pl.loop(1, middle)
    def _(step):
        send(middle + step)
        send(middle - step)


def unpack_kernel(gi_hbm, final, gi_out, gw_ref, gb_ref, flat, sem):
    move = pltpu.make_async_copy(gi_hbm, gi_out, sem)
    move.start()
    for block in range(112):
        flat[block * 4 : block * 4 + 4] = final[block]
    for spot, dz in enumerate((0, 2, 1)):
        for dx in range(3):
            start = spot * 96 + dx * 32
            for dy in range(2):
                gw_ref[9 * dz + 3 * dy + dx] = flat[start : start + 32, dy * 64 : dy * 64 + 64]
            for row in (start, start + 16):
                lane, line = (row // 144) * 64, 288 + row % 144
                gw_ref[9 * dz + 6 + dx, row - start : row - start + 16] = flat[
                    line : line + 16, lane : lane + 64
                ]
    gb_ref[...] = flat[432:433, 64:128]
    move.wait()


def fused_kernel(
    n,
    factor,
    a_hbm,
    g_hbm,
    w_hbm,
    gi_hbm,
    final_hbm,
    a_own,
    a_halo,
    g_own,
    g_halo,
    w_own,
    g_pad,
    a_stack,
    w_rows,
    acc,
    flat,
    first,
    second,
    third,
    partial,
    result,
    gi_own,
    load_sem,
    keep_sem,
    swap_sem,
    halo_send,
    halo_recv,
    send_sem,
    recv_sem,
):
    in_chan, planes, rows, lanes = a_own.shape
    chans = g_own.shape[0]
    slabs = 2 * n
    share = chans // slabs
    half = n // 2
    members = 2 * n
    scale = first.shape[0] // (7 * members)
    units = (3 * scale, 2 * scale, 2 * scale)
    base = (0, 3 * scale, 5 * scale)
    slab, sample = lax.axis_index("slab"), lax.axis_index("sample")
    core = lax.rem(sample, 2)
    place = (
        lax.div(slab, n) * half + lax.rem(lax.div(sample, 2), half),
        lax.rem(slab, n),
        lax.div(sample, n),
    )
    own = [place[part] * 2 + core for part in range(3)]

    def device(axis, coordinate, other):
        x, y, z = (coordinate if axis == i else place[i] for i in range(3))
        return {
            "slab": lax.div(x, half) * n + y,
            "sample": z * n + lax.rem(x, half) * 2 + other,
        }

    def wide(axis, step):
        index = lax.rem(own[axis] + step, members)
        return index, device(axis, lax.div(index, 2), lax.rem(index, 2))

    def narrow(axis, step):
        index = lax.rem(place[axis] + step, n)
        return index, device(axis, index, core)

    load_a = pltpu.make_async_copy(a_hbm, a_own, load_sem.at[0])
    load_w = pltpu.make_async_copy(w_hbm, w_own, load_sem.at[1])
    load_g = pltpu.make_async_copy(
        g_hbm.at[:, pl.ds(slab * planes, planes)],
        g_own.at[pl.ds(slab * share, share)],
        load_sem.at[2],
    )
    load_a.start()
    load_w.start()
    load_g.start()

    barrier = pltpu.get_barrier_semaphore()

    column, side = lax.rem(slab, n), lax.div(slab, n)

    def other_slab(cross, step):
        return lax.rem(side + cross, 2) * n + lax.rem(column + step, n)

    def greet(peer):
        pl.semaphore_signal(barrier, inc=1, device_id=peer, device_id_type=MESH)

    def greet_step(step):
        greet({"slab": other_slab(1, step)})
        for axis in range(3):
            index = lax.rem(place[axis] + step, n)
            greet(device(axis, index, core))
            greet(device(axis, index, 1 - core))

    far_out(half, greet_step)

    greet(device(0, place[0], 1 - core))
    pl.semaphore_wait(barrier, 7 * (n - 1) + 1)

    def whole(buffer, count, sem):
        view = buffer.at[pl.ds(0, count)]
        pltpu.make_async_copy(view, view, sem).wait()

    def swap(cross, step):
        target = other_slab(cross, step)
        pltpu.make_async_remote_copy(
            src_ref=g_hbm.at[:, pl.ds(target * planes, planes)],
            dst_ref=g_own.at[pl.ds(slab * share, share)],
            send_sem=swap_sem.at[0],
            recv_sem=swap_sem.at[1],
            device_id={"slab": target},
            device_id_type=MESH,
        ).start()

    def halo_copy(source, target, which, side, peer):
        return pltpu.make_async_remote_copy(
            src_ref=source,
            dst_ref=target,
            send_sem=halo_send.at[which, side],
            recv_sem=halo_recv.at[which, side],
            device_id={"slab": peer},
            device_id_type=MESH,
        )

    def halo_pair(source, target, which):
        up = halo_copy(source.at[:, planes - 1], target.at[0], which, 0, lax.rem(slab + 1, slabs))
        down = halo_copy(source.at[:, 0], target.at[1], which, 1, lax.rem(slab + slabs - 1, slabs))
        return up, down

    def halo_start(pair):
        pl.when(slab < slabs - 1)(pair[0].start)
        pl.when(slab > 0)(pair[1].start)

    def halo_arrive(pair, target):
        @pl.when(slab > 0)
        def _():
            pair[0].wait_recv()

        @pl.when(slab == 0)
        def _():
            target[0] = jnp.zeros(target.shape[1:], target.dtype)

        @pl.when(slab < slabs - 1)
        def _():
            pair[1].wait_recv()

        @pl.when(slab == slabs - 1)
        def _():
            target[1] = jnp.zeros(target.shape[1:], target.dtype)

    def halo_sent(pair):
        pl.when(slab < slabs - 1)(pair[0].wait_send)
        pl.when(slab > 0)(pair[1].wait_send)

    load_a.wait()
    a_pair = halo_pair(a_own, a_halo, 0)
    halo_start(a_pair)

    far_first = sorted(range(n), key=lambda step: -min(step, n - step))
    for step in far_first:
        swap(1, step)
        if step:
            swap(0, step)

    for z in range(planes + 2):
        g_pad[z, 0] = jnp.zeros((chans, lanes), BF16)
        g_pad[z, rows + 1] = jnp.zeros((chans, lanes), BF16)

    tail = lax.broadcasted_iota(jnp.int32, (rows, 32, lanes), 1) == 0

    def stack_plane(z, plane):
        cells = jnp.swapaxes(plane.astype(F32), 0, 1)
        stack = [lane_shift(cells, 1), cells, lane_shift(cells, -1), jnp.where(tail, 1.0, 0.0)]
        for part, value in enumerate(stack):
            a_stack[z, :, part * 32 : part * 32 + 32] = value.astype(BF16)

    def pad_plane(z, plane):
        g_pad[z, 1 : rows + 1] = jnp.swapaxes(plane.astype(F32), 0, 1).astype(BF16)

    for z in range(planes):
        stack_plane(z + 1, a_own[:, z])
    load_w.wait()
    for zy in range(9):
        for dx in range(3):
            w_rows[dx * 32 : dx * 32 + 32, zy * chans : (zy + 1) * chans] = w_own[3 * zy + dx]
    halo_arrive(a_pair, a_halo)
    stack_plane(0, a_halo[0])
    stack_plane(planes + 1, a_halo[1])

    load_g.wait()
    whole(g_own, chans - share, swap_sem.at[1])
    g_pair = halo_pair(g_own, g_halo, 1)
    halo_start(g_pair)
    for z in range(planes):
        pad_plane(z + 1, g_own[:, z])

    total = None
    for z in range(planes):
        cot = jnp.concatenate(
            [
                jnp.concatenate([g_pad[z + 1, y + 1 - dy] for y in range(rows)], axis=1)
                for dy in (-1, 0, 1)
            ],
            axis=0,
        )
        cells = jnp.concatenate(
            [
                jnp.concatenate([a_stack[z + 1 + dz, y, :height] for y in range(rows)], axis=1)
                for dz, height in ((-1, 96), (1, 96), (0, 112))
            ],
            axis=0,
        )
        term = lax.dot_general(
            cells, cot, (((1,), (1,)), ((), ())), preferred_element_type=F32
        )
        if z == 0:
            acc[:, 0:192] = term
        else:
            acc[:, 0:192] += term
    low = lax.broadcasted_iota(jnp.int32, (144, 128), 1) < 64
    flat[0:144] = jnp.where(low, acc[0:144, 128:256], pltpu.roll(acc[144:288, 128:256], 64, 1))
    for block in range(112):
        if block < 72:
            partial[block] = acc[block * 4 : block * 4 + 4, 0:128]
        elif block < 108:
            partial[block] = flat[block * 4 - 288 : block * 4 - 284]
        else:
            partial[block] = acc[block * 4 - 144 : block * 4 - 140, 0:128]

    def copy(source, target, phase, part, peer):
        return pltpu.make_async_remote_copy(
            src_ref=source,
            dst_ref=target,
            send_sem=send_sem.at[phase, part],
            recv_sem=recv_sem.at[phase, part],
            device_id=peer,
            device_id_type=MESH,
        )

    def piece(part, index, count=members):
        return pl.ds(base[part] * count + index * units[part], units[part])

    def scatter(step):
        for part in range(3):
            index, peer = wide(part, step)
            copy(
                partial.at[piece(part, index)], first.at[piece(part, own[part])], 0, part, peer
            ).start()

    far_out(n, scatter)

    def inputs_plane(z):
        outs = []
        for y in range(0, rows, 2):
            stacked = jnp.concatenate(
                [
                    jnp.concatenate(
                        [g_pad[z + 1 - dz, y + 1 - dy], g_pad[z + 1 - dz, y + 2 - dy]], axis=1
                    )
                    for dz in (-1, 0, 1)
                    for dy in (-1, 0, 1)
                ],
                axis=0,
            )
            mixed = jnp.dot(w_rows[...], stacked, preferred_element_type=F32)
            for side in range(2):
                part = mixed[:, side * lanes : (side + 1) * lanes]
                outs.append(
                    part[32:64] + lane_shift(part[0:32], -1) + lane_shift(part[64:96], 1)
                )
        gi_own[:, z] = jnp.swapaxes(jnp.stack(outs), 0, 1).astype(BF16)

    for z in range(1, planes - 1):
        inputs_plane(z)

    def add_up(buffer, part, count):
        total = buffer[piece(part, 0, count)]
        for index in range(1, count):
            total = total + buffer[piece(part, index, count)]
        return total

    for part in range(3):
        first[piece(part, own[part])] = partial[piece(part, own[part])]
        whole(first, (members - 1) * units[part], recv_sem.at[0, part])
        axis = (part + 1) % 3
        mine = piece(part, place[axis], n)
        second[mine] = add_up(first, part, members)

        def spread(step, part=part, axis=axis, mine=mine):
            copy(second.at[mine], second.at[mine], 1, part, narrow(axis, step)[1]).start()

        far_out(half, spread)

    halo_arrive(g_pair, g_halo)
    pad_plane(0, g_halo[0])
    pad_plane(planes + 1, g_halo[1])
    inputs_plane(0)
    inputs_plane(planes - 1)
    save_gi = pltpu.make_async_copy(gi_own, gi_hbm, keep_sem.at[3])
    save_gi.start()

    for part in range(3):
        whole(second, (n - 1) * units[part], recv_sem.at[1, part])
        axis = (part + 2) % 3
        mine = piece(part, place[axis], n)
        third[mine] = add_up(second, part, n)

        def spread(step, part=part, axis=axis, mine=mine):
            copy(third.at[mine], third.at[mine], 2, part, narrow(axis, step)[1]).start()

        far_out(half, spread)

    for part in range(3):
        whole(first, (members - 1) * units[part], send_sem.at[0, part])

    keep_own = [
        pltpu.make_async_copy(
            result.at[piece(part, own[part])],
            final_hbm.at[piece(part, own[part])],
            keep_sem.at[part],
        )
        for part in range(3)
    ]

    for part in range(3):
        whole(third, (n - 1) * units[part], recv_sem.at[2, part])
        mine = piece(part, own[part])
        result[mine] = add_up(third, part, n) * factor
        keep_own[part].start()

        def spread(step, part=part, mine=mine):
            copy(result.at[mine], final_hbm.at[mine], 3, part, wide(part, step)[1]).start()

        far_out(n, spread)

    for part in range(3):
        whole(final_hbm, (members - 1) * units[part], recv_sem.at[3, part])

    for part in range(3):
        keep_own[part].wait()
    save_gi.wait()
    whole(g_own, chans - share, swap_sem.at[0])
    halo_sent(a_pair)
    halo_sent(g_pair)
    for part in range(3):
        whole(second, (n - 1) * units[part], send_sem.at[1, part])
        whole(third, (n - 1) * units[part], send_sem.at[2, part])
        whole(first, (members - 1) * units[part], send_sem.at[3, part])


def local(activations, grad_out, weight):
    slabs, samples = lax.axis_size("slab"), lax.axis_size("sample")
    n = slabs // 2
    _, in_chan, planes, rows, lanes = activations.shape
    chans = weight.shape[1]
    cells = samples * slabs * planes * rows * lanes
    vmem = pl.BlockSpec(memory_space=pltpu.VMEM)
    hbm = pl.BlockSpec(memory_space=pltpu.HBM)
    weight = weight.transpose(0, 2, 1)
    grad_in, packed = pl.pallas_call(
        functools.partial(fused_kernel, n, 1.0 / math.sqrt(cells)),
        out_shape=(
            jax.ShapeDtypeStruct(activations.shape[1:], BF16),
            jax.ShapeDtypeStruct((112, 4, 128), F32),
        ),
        in_specs=[hbm] * 3,
        out_specs=(hbm, hbm),
        scratch_shapes=[
            pltpu.VMEM((in_chan, planes, rows, lanes), BF16),
            pltpu.VMEM((2, in_chan, rows, lanes), BF16),
            pltpu.VMEM((chans, planes, rows, lanes), BF16),
            pltpu.VMEM((2, chans, rows, lanes), BF16),
            pltpu.VMEM(weight.shape, BF16),
            pltpu.VMEM((planes + 2, rows + 2, chans, lanes), BF16),
            pltpu.VMEM((planes + 2, rows, 128, lanes), BF16),
            pltpu.VMEM((96, 9 * chans), BF16),
            pltpu.VMEM((304, 256), F32),
            pltpu.VMEM((448, 128), F32),
            pltpu.VMEM((112, 4, 128), F32),
            pltpu.VMEM((56, 4, 128), F32),
            pltpu.VMEM((56, 4, 128), F32),
            pltpu.VMEM((112, 4, 128), F32),
            pltpu.VMEM((112, 4, 128), F32),
            pltpu.VMEM(activations.shape[1:], BF16),
            pltpu.SemaphoreType.DMA((3,)),
            pltpu.SemaphoreType.DMA((4,)),
            pltpu.SemaphoreType.DMA((2,)),
            pltpu.SemaphoreType.DMA((2, 2)),
            pltpu.SemaphoreType.DMA((2, 2)),
            pltpu.SemaphoreType.DMA((4, 3)),
            pltpu.SemaphoreType.DMA((4, 3)),
        ],
        compiler_params=pltpu.CompilerParams(
            collective_id=0, has_side_effects=True, vmem_limit_bytes=58 << 20
        ),
        name="backward",
    )(activations[0], grad_out[0], weight)
    grad_in, gw, gb = pl.pallas_call(
        unpack_kernel,
        out_shape=(
            jax.ShapeDtypeStruct(activations.shape[1:], BF16),
            jax.ShapeDtypeStruct(weight.shape, F32),
            jax.ShapeDtypeStruct((1, chans), F32),
        ),
        in_specs=[hbm, vmem],
        out_specs=(hbm, vmem, vmem),
        scratch_shapes=[pltpu.VMEM((448, 128), F32), pltpu.SemaphoreType.DMA],
        name="unpack",
    )(grad_in, packed)
    return grad_in[None], gw.transpose(0, 2, 1), gb[0]


def solution(mesh):
    placed = (P("sample", None, "slab", None, None), P("sample", "slab", None, None, None), P())
    return jax.shard_map(
        local,
        mesh=mesh,
        in_specs=placed,
        out_specs=(P("sample", None, "slab", None, None), P(), P()),
        check_vma=False,
    )
```

time: 480 us -> 75.8 us (0.16)
  waiting for transfers between devices: 288 us -> 0 us
  blocking collectives: 132 us -> 0 us
  Pallas kernels: 0 us -> 75 us
  starting transfers between devices: 21.1 us -> 0 us
  matrix products: 16.3 us -> 0 us
  between operations: 14.2 us -> 0.64 us
    psum x1 -> x0, waiting for transfers between devices: 280 us -> none  [local(): wtotal, btotal = lax.psum((wpart, bpart), ('slab', 'sample'))]
    psum x1 -> x0, blocking collectives: 132 us -> none  [local(): wtotal, btotal = lax.psum((wpart, bpart), ('slab', 'sample'))]
    pallas_call x0 -> x2, Pallas kernels: none -> 75 us  [the longest x1 64.3 us: local(): pl.pallas_call(functools.partial(fused_kernel, n, 1.0 / math.sqrt(cells))...]
    dot_general x54 -> x0, matrix products: 16.3 us -> none  [the longest x27 8.22 us: local(): jnp.einsum('oi,sozyx->sizyx', weight[offset], moved_co, preferred_element...]
    all_to_all x1 -> x0, starting transfers between devices: 13.1 us -> none  [local(): lax.all_to_all(grad_out, 'slab', split_axis=2, concat_axis=1, tiled=True)]
    ppermute x4 -> x0, waiting for transfers between devices: 8.66 us -> none  [the longest x2 8.3 us: with_halo(): lax.ppermute(lax.slice_in_dim(block, 0, width, axis=dim), axis, backward)]
    ppermute x4 -> x0, starting transfers between devices: 7.97 us -> none  [the longest x2 5.2 us: with_halo(): lax.ppermute(lax.slice_in_dim(block, block.shape[dim] - width, None, axis...]
  transfers between devices with their start and end apart: 6 -> 0, of which waited for: 3 -> 0; matrix products, arithmetic and copies ran while one was open for 2% -> 0% of each run, Pallas kernels for 0% -> 0%
where the time goes in v2:
time: 75.8 us; the launch traced here: 75.7 us
  Pallas kernels  75 us (99%)
    pallas_call x1, Pallas kernels, local(): pl.pallas_call(functools.partial(fused_kernel, n, 1.0 / math.sqrt(cells))...  64.3 us
    pallas_call x1, Pallas kernels, local(): pl.pallas_call(unpack_kernel, out_shape=(jax.ShapeDtypeStruct(activations...  10.8 us

profile of v2, /device:TPU:1, one launch (start us, length us, event | category | flops | bytes accessed | tf_op | source)
XLA Modules:
  0.0 75.7 jit_solution(5946873462980298327)
XLA Ops:
  0.6 64.3 %backward.1 = (bf16[32,4,8,128]{3,2,1,0:T(8,128)(2,1)}, f32[112,4,128]{2,1,0:T(4,128)}) custom-call(bf16[32,4,8,128]{3,2,1,0:T(8,128)(2,1)} %bitcast.7, bf16[4,64,8,128]{3,2,1,0:T(8,128)(2,1)} %bitcast.6, bf16[27,32,64]{2,1,0:T(8,128)(2,1)} %bitcast.8), custom_call_target="tpu_custom_call" | custom-call | tf_op jit(solution)/shard_map/backward/pallas_call | solution.py:409
  64.9 10.8 %unpack.1 = (bf16[32,4,8,128]{3,2,1,0:T(8,128)(2,1)}, f32[27,32,64]{2,1,0:T(8,128)}, f32[1,64]{1,0:T(1,128)}) custom-call(bf16[32,4,8,128]{3,2,1,0:T(8,128)(2,1)} %get-tuple-element.8.gi_hbm, f32[112,4,128]{2,1,0:T(4,128)} %get-tuple-element.9.final), custom_call_target="tpu_custom_call" | custom-call | tf_op jit(solution)/shard_map/unpack/pallas_call | solution.py:447

commit v3 on v2

--- a/solution.py
+++ b/solution.py
@@ -29,9 +29,8 @@
         send(middle - step)
 
 
-def unpack_kernel(gi_hbm, final, gi_out, gw_ref, gb_ref, flat, sem):
-    move = pltpu.make_async_copy(gi_hbm, gi_out, sem)
-    move.start()
+def unpack_kernel(gi_hbm, final, gi_out, gw_ref, gb_ref, flat):
+    gi_out[...] = gi_hbm[...]
     for block in range(112):
         flat[block * 4 : block * 4 + 4] = final[block]
     for spot, dz in enumerate((0, 2, 1)):
@@ -45,7 +44,6 @@
                     line : line + 16, lane : lane + 64
                 ]
     gb_ref[...] = flat[432:433, 64:128]
-    move.wait()
 
 
 def fused_kernel(
@@ -451,9 +449,9 @@
             jax.ShapeDtypeStruct(weight.shape, F32),
             jax.ShapeDtypeStruct((1, chans), F32),
         ),
-        in_specs=[hbm, vmem],
-        out_specs=(hbm, vmem, vmem),
-        scratch_shapes=[pltpu.VMEM((448, 128), F32), pltpu.SemaphoreType.DMA],
+        in_specs=[vmem, vmem],
+        out_specs=(vmem, vmem, vmem),
+        scratch_shapes=[pltpu.VMEM((448, 128), F32)],
         name="unpack",
     )(grad_in, packed)
     return grad_in[None], gw.transpose(0, 2, 1), gb[0]

time: 75.8 us -> 67 us (0.88)
  Pallas kernels: 75 us -> 66.2 us
    pallas_call x1, Pallas kernels: 10.8 us -> 1.94 us  [local(): pl.pallas_call(unpack_kernel, out_shape=(jax.ShapeDtypeStruct(activations...]
where the time goes in v3:
time: 67 us; the launch traced here: 66.8 us
  Pallas kernels  66.2 us (99%)
    pallas_call x1, Pallas kernels, local(): pl.pallas_call(functools.partial(fused_kernel, n, 1.0 / math.sqrt(cells))...  64.3 us
    pallas_call x1, Pallas kernels, local(): pl.pallas_call(unpack_kernel, out_shape=(jax.ShapeDtypeStruct(activations...  1.94 us

profile of v3, /device:TPU:1, one launch (start us, length us, event | category | flops | bytes accessed | tf_op | source)
XLA Modules:
  0.0 66.8 jit_solution(6068392876481655506)
XLA Ops:
  0.6 64.3 %backward.1 = (bf16[32,4,8,128]{3,2,1,0:T(8,128)(2,1)}, f32[112,4,128]{2,1,0:T(4,128)}) custom-call(bf16[32,4,8,128]{3,2,1,0:T(8,128)(2,1)} %bitcast.7, bf16[4,64,8,128]{3,2,1,0:T(8,128)(2,1)} %bitcast.6, bf16[27,32,64]{2,1,0:T(8,128)(2,1)} %bitcast.8), custom_call_target="tpu_custom_call" | custom-call | tf_op jit(solution)/shard_map/backward/pallas_call | solution.py:407
  64.9 1.9 %unpack.1 = (bf16[32,4,8,128]{3,2,1,0:T(8,128)(2,1)}, f32[27,32,64]{2,1,0:T(8,128)}, f32[1,64]{1,0:T(1,128)}) custom-call(bf16[32,4,8,128]{3,2,1,0:T(8,128)(2,1)} %get-tuple-element.8.gi_hbm, f32[112,4,128]{2,1,0:T(4,128)} %get-tuple-element.9.final), custom_call_target="tpu_custom_call" | custom-call | tf_op jit(solution)/shard_map/unpack/pallas_call | solution.py:445

commit v4 on v3

--- a/solution.py
+++ b/solution.py
@@ -237,7 +237,6 @@
     load_g.wait()
     whole(g_own, chans - share, swap_sem.at[1])
     g_pair = halo_pair(g_own, g_halo, 1)
-    halo_start(g_pair)
     for z in range(planes):
         pad_plane(z + 1, g_own[:, z])
 
@@ -295,6 +294,7 @@
             ).start()
 
     far_out(n, scatter)
+    halo_start(g_pair)
 
     def inputs_plane(z):
         outs = []
@@ -338,6 +338,41 @@
 
         far_out(half, spread)
 
+
+    for part in range(3):
+        whole(second, (n - 1) * units[part], recv_sem.at[1, part])
+        axis = (part + 2) % 3
+        mine = piece(part, place[axis], n)
+        third[mine] = add_up(second, part, n)
+
+        def spread(step, part=part, axis=axis, mine=mine):
+            copy(third.at[mine], third.at[mine], 2, part, narrow(axis, step)[1]).start()
+
+        far_out(half, spread)
+
+    for part in range(3):
+        whole(first, (members - 1) * units[part], send_sem.at[0, part])
+
+    keep_own = [
+        pltpu.make_async_copy(
+            result.at[piece(part, own[part])],
+            final_hbm.at[piece(part, own[part])],
+            keep_sem.at[part],
+        )
+        for part in range(3)
+    ]
+
+    for part in range(3):
+        whole(third, (n - 1) * units[part], recv_sem.at[2, part])
+        mine = piece(part, own[part])
+        result[mine] = add_up(third, part, n) * factor
+        keep_own[part].start()
+
+        def spread(step, part=part, mine=mine):
+            copy(result.at[mine], final_hbm.at[mine], 3, part, wide(part, step)[1]).start()
+
+        far_out(n, spread)
+
     halo_arrive(g_pair, g_halo)
     pad_plane(0, g_halo[0])
     pad_plane(planes + 1, g_halo[1])
@@ -345,40 +380,6 @@
     inputs_plane(planes - 1)
     save_gi = pltpu.make_async_copy(gi_own, gi_hbm, keep_sem.at[3])
     save_gi.start()
-
-    for part in range(3):
-        whole(second, (n - 1) * units[part], recv_sem.at[1, part])
-        axis = (part + 2) % 3
-        mine = piece(part, place[axis], n)
-        third[mine] = add_up(second, part, n)
-
-        def spread(step, part=part, axis=axis, mine=mine):
-            copy(third.at[mine], third.at[mine], 2, part, narrow(axis, step)[1]).start()
-
-        far_out(half, spread)
-
-    for part in range(3):
-        whole(first, (members - 1) * units[part], send_sem.at[0, part])
-
-    keep_own = [
-        pltpu.make_async_copy(
-            result.at[piece(part, own[part])],
-            final_hbm.at[piece(part, own[part])],
-            keep_sem.at[part],
-        )
-        for part in range(3)
-    ]
-
-    for part in range(3):
-        whole(third, (n - 1) * units[part], recv_sem.at[2, part])
-        mine = piece(part, own[part])
-        result[mine] = add_up(third, part, n) * factor
-        keep_own[part].start()
-
-        def spread(step, part=part, mine=mine):
-            copy(result.at[mine], final_hbm.at[mine], 3, part, wide(part, step)[1]).start()
-
-        far_out(n, spread)
 
     for part in range(3):
         whole(final_hbm, (members - 1) * units[part], recv_sem.at[3, part])

time: 67 us -> 65.7 us (0.981)
  Pallas kernels: 66.2 us -> 64.9 us
    pallas_call x1, Pallas kernels: 64.3 us -> 62.9 us  [local(): pl.pallas_call(functools.partial(fused_kernel, n, 1.0 / math.sqrt(cells))...]
where the time goes in v4:
time: 65.7 us; the launch traced here: 65.5 us
  Pallas kernels  64.9 us (99%)
    pallas_call x1, Pallas kernels, local(): pl.pallas_call(functools.partial(fused_kernel, n, 1.0 / math.sqrt(cells))...  62.9 us
    pallas_call x1, Pallas kernels, local(): pl.pallas_call(unpack_kernel, out_shape=(jax.ShapeDtypeStruct(activations...  1.94 us

profile of v4, /device:TPU:1, one launch (start us, length us, event | category | flops | bytes accessed | tf_op | source)
XLA Modules:
  0.0 65.5 jit_solution(11764274535284640082)
XLA Ops:
  0.6 62.9 %backward.1 = (bf16[32,4,8,128]{3,2,1,0:T(8,128)(2,1)}, f32[112,4,128]{2,1,0:T(4,128)}) custom-call(bf16[32,4,8,128]{3,2,1,0:T(8,128)(2,1)} %bitcast.7, bf16[4,64,8,128]{3,2,1,0:T(8,128)(2,1)} %bitcast.6, bf16[27,32,64]{2,1,0:T(8,128)(2,1)} %bitcast.8), custom_call_target="tpu_custom_call" | custom-call | tf_op jit(solution)/shard_map/backward/pallas_call | solution.py:408
  63.6 1.9 %unpack.1 = (bf16[32,4,8,128]{3,2,1,0:T(8,128)(2,1)}, f32[27,32,64]{2,1,0:T(8,128)}, f32[1,64]{1,0:T(1,128)}) custom-call(bf16[32,4,8,128]{3,2,1,0:T(8,128)(2,1)} %get-tuple-element.8.gi_hbm, f32[112,4,128]{2,1,0:T(4,128)} %get-tuple-element.9.final), custom_call_target="tpu_custom_call" | custom-call | tf_op jit(solution)/shard_map/unpack/pallas_call | solution.py:446

commit v5 on v4

--- a/solution.py
+++ b/solution.py
@@ -118,9 +118,6 @@
         g_own.at[pl.ds(slab * share, share)],
         load_sem.at[2],
     )
-    load_a.start()
-    load_w.start()
-    load_g.start()
 
     barrier = pltpu.get_barrier_semaphore()
 
@@ -142,6 +139,9 @@
     far_out(half, greet_step)
 
     greet(device(0, place[0], 1 - core))
+    load_a.start()
+    load_w.start()
+    load_g.start()
     pl.semaphore_wait(barrier, 7 * (n - 1) + 1)
 
     def whole(buffer, count, sem):
@@ -199,15 +199,14 @@
         pl.when(slab < slabs - 1)(pair[0].wait_send)
         pl.when(slab > 0)(pair[1].wait_send)
 
-    load_a.wait()
-    a_pair = halo_pair(a_own, a_halo, 0)
-    halo_start(a_pair)
-
     far_first = sorted(range(n), key=lambda step: -min(step, n - step))
     for step in far_first:
         swap(1, step)
         if step:
             swap(0, step)
+    load_a.wait()
+    a_pair = halo_pair(a_own, a_halo, 0)
+    halo_start(a_pair)
 
     for z in range(planes + 2):
         g_pad[z, 0] = jnp.zeros((chans, lanes), BF16)

time: 65.7 us -> 68.3 us (1.040)
  Pallas kernels: 64.9 us -> 67.5 us
    pallas_call x1, Pallas kernels: 62.9 us -> 65.5 us  [local(): pl.pallas_call(functools.partial(fused_kernel, n, 1.0 / math.sqrt(cells))...]
where the time goes in v5:
time: 68.3 us; the launch traced here: 68.1 us
  Pallas kernels  67.5 us (99%)
    pallas_call x1, Pallas kernels, local(): pl.pallas_call(functools.partial(fused_kernel, n, 1.0 / math.sqrt(cells))...  65.5 us
    pallas_call x1, Pallas kernels, local(): pl.pallas_call(unpack_kernel, out_shape=(jax.ShapeDtypeStruct(activations...  1.94 us

profile of v5, /device:TPU:1, one launch (start us, length us, event | category | flops | bytes accessed | tf_op | source)
XLA Modules:
  0.0 68.1 jit_solution(14345601348865262080)
XLA Ops:
  0.6 65.5 %backward.1 = (bf16[32,4,8,128]{3,2,1,0:T(8,128)(2,1)}, f32[112,4,128]{2,1,0:T(4,128)}) custom-call(bf16[32,4,8,128]{3,2,1,0:T(8,128)(2,1)} %bitcast.7, bf16[4,64,8,128]{3,2,1,0:T(8,128)(2,1)} %bitcast.6, bf16[27,32,64]{2,1,0:T(8,128)(2,1)} %bitcast.8), custom_call_target="tpu_custom_call" | custom-call | tf_op jit(solution)/shard_map/backward/pallas_call | solution.py:407
  66.2 1.9 %unpack.1 = (bf16[32,4,8,128]{3,2,1,0:T(8,128)(2,1)}, f32[27,32,64]{2,1,0:T(8,128)}, f32[1,64]{1,0:T(1,128)}) custom-call(bf16[32,4,8,128]{3,2,1,0:T(8,128)(2,1)} %get-tuple-element.8.gi_hbm, f32[112,4,128]{2,1,0:T(4,128)} %get-tuple-element.9.final), custom_call_target="tpu_custom_call" | custom-call | tf_op jit(solution)/shard_map/unpack/pallas_call | solution.py:445
